TPU v7x, 32 devices: a whole 2x2x4 slice. The times are simulated.
32 devices in a mesh: tm: 16 (over z, x, core), chan: 2 (over y).
Axes of the slice: x: 2, y: 2, z: 4, core: 2. Of those that a mesh axis runs over, the one named last changes fastest.
Arguments:
- series: float32 [64, 8192], P('chan', 'tm'), may hold values from -200 to 200
- tail: float32 [64, 127], P('chan'), may hold values from -200 to 200
- excl: int32 [1], replicated, may hold values from 32 to 128
Outputs:
- profile: float32 [8192], P('tm')
All inputs are finite; a program needn't handle non-finite values.
Results may differ from a plain program's by a relative error of at most 0.0003.
Values may be sent and summed in bfloat16 or wider, within the bound.
No kernel may reach another device: no remote copies, remote signals or barrier semaphores. Data moves between devices by JAX's collectives and lax.ppermute only.
A program may use at most 128 MiB of HBM per device.

v0:
```python
import math
import jax
import jax.numpy as jnp
from jax import lax
from jax.sharding import PartitionSpec as P

C = 64
EPSILON = 1e-05
CEILING = 4.0


def from_behind(shard, axis, by):
    length = lax.axis_size(axis)
    pairs = [(i, i + by) for i in range(length) if 0 <= i + by < length]
    return lax.ppermute(shard, axis, pairs)


def normalize(extended, count, length, channels):
    starts = (
        jnp.arange(length, dtype=jnp.int32)[:, None] + jnp.arange(count, dtype=jnp.int32)[None, :]
    )
    windows = extended[:, starts]
    center = jnp.mean(windows, axis=1, keepdims=True)
    shifted = windows - center
    spread = jnp.mean(shifted * shifted, axis=1, keepdims=True)
    factor = lax.rsqrt(spread + EPSILON) * (1.0 / math.sqrt(length * channels))
    return (shifted * factor).astype(jnp.bfloat16)


def correlate(left, right):
    return lax.dot_general(
        left, right, (((0, 1), (0, 1)), ((), ())), preferred_element_type=jnp.float32
    )


def on_device(series, tail, excl):
    count = series.shape[1]
    width = tail.shape[1]
    length = width + 1
    blocks = lax.axis_size("tm")
    block_index = lax.axis_index("tm")
    head = from_behind(series[:, :width], "tm", -1)
    head = jnp.where(block_index == blocks - 1, tail, head)
    extended = jnp.concatenate([series, head], axis=1)
    query = normalize(extended, count, length, C)
    nearby = from_behind(query, "tm", -1)
    faraway = from_behind(query, "tm", -2)
    limit = excl[0]

    def scored(total, row_pos, offset):
        columns = (block_index + offset) * count + jnp.arange(count, dtype=jnp.int32)[None, :]
        keep = (jnp.abs(row_pos - columns) >= limit) & (block_index + offset < blocks)
        return jnp.where(keep, 1.0 - total, CEILING)

    row_pos = block_index * count + jnp.arange(count, dtype=jnp.int32)[:, None]

    def summed(right, offset):
        total = lax.psum(correlate(query, right), "chan")
        return scored(total, row_pos, offset)

    own_scores = summed(query, 0)
    near_scores = summed(nearby, 1)
    far_scores = summed(faraway, 2)
    row_best = jnp.minimum(
        jnp.min(own_scores, axis=1),
        jnp.minimum(jnp.min(near_scores, axis=1), jnp.min(far_scores, axis=1)),
    )
    near_cols = jnp.min(near_scores, axis=0)
    far_cols = jnp.min(far_scores, axis=0)
    near_home = from_behind(CEILING - near_cols, "tm", 1)
    far_home = from_behind(CEILING - far_cols, "tm", 2)
    return jnp.minimum(row_best, jnp.minimum(CEILING - near_home, CEILING - far_home))


def solution(mesh):
    placed = (P("chan", "tm"), P("chan", None), P())
    return jax.shard_map(on_device, mesh=mesh, in_specs=placed, out_specs=P("tm"), check_vma=False)
```

profile of v0, /device:TPU:9, one launch (start us, length us, event | category | flops | bytes accessed | tf_op | source)
XLA Modules:
  0.0 510.5 jit_solution(10372994987045576951)
XLA Ops:
  6.5 0.0 all-reduce.3.cloned.1.call-start
  6.5 0.7 slice.3
  7.3 2.6 collective-permute-start
  9.9 0.1 copy.27
  10.0 2.3 collective-permute-done
  12.3 0.8 pad_maximum_fusion
  13.2 0.2 copy.18
  13.4 215.5 %gather_fusion = f32[65536,32]{1,0:T(8,128)} fusion(f32[32,639]{0,1:T(8,128)S(1)} %copy.18, s32[65536]{0:T(1024)S(1)} %broadcast_clamp_fusion), kind=kCustom, calls=%fused_computation | custom fusion | bytes 17039360 | tf_op jit(solution)/shard_map/gather | solution.py:22
  228.9 22.1 %copy.26 = f32[128,512,32]{1,0,2:T(8,128)} copy(f32[128,512,32]{2,1,0:T(8,128)} %bitcast.26) | data formatting | bytes 16777216 | tf_op jit(solution)/shard_map/gather | solution.py:22
  251.0 0.0 copy-start
  251.0 4.7 bitcast_reduce_fusion
  255.7 1.0 copy-done
  256.7 1.4 multiply_reduce_fusion
  258.2 1.7 multiply_convert_fusion
  259.9 1.9 collective-permute-start.1
  261.8 4.0 collective-permute-start.2
  265.9 3.4 convolution_bitcast_fusion.2
  269.3 83.4 %collective-permute-done.1 = bf16[32,128,512]{2,1,0:T(8,128)(2,1)S(1)} collective-permute-done((bf16[32,128,512]{2,1,0:T(8,128)(2,1)S(1)}, bf16[32,128,512]{2,1,0:T(8,128)(2,1)S(1)}, u32[]{:S(2)}, u32[]{:S(2)}) %collective-permute-start.1) | collective-permute-done | bytes 4194336 | tf_op jit(solution)/shard_map/ppermute | solution.py:15
  352.7 3.4 convolution_bitcast_fusion.1
  356.1 0.9 collective-permute-done.2
  356.9 3.4 convolution_bitcast_fusion
  360.3 0.0 all-reduce.3.cloned.1.call-update
  361.0 129.8 %all-reduce.3.cloned.1.call-done = (f32[512,512]{1,0:T(8,128)}, f32[512,512]{1,0:T(8,128)}, f32[512,512]{1,0:T(8,128)}) async-done(((f32[512,512]{1,0:T(8,128)}, f32[512,512]{1,0:T(8,128)}, f32[512,512]{1,0:T(8,128)}), (f32[512,512]{1,0:T(8,128)}, f32[512,512]{1,0:T(8,128)}, f32[512,512]{1,0:T(8,128)})) %all-reduce.3.cloned.1.call-update) | async-done | bytes 3145744 | tf_op jit(solution)/shard_map/psum | solution.py:58
  490.8 3.2 fusion.6
  494.0 3.8 collective-permute-start.3
  497.8 3.1 collective-permute-start.4
  500.9 0.0 collective-permute-done.3
  500.9 2.1 collective-permute-done.4
  503.0 0.6 minimum_minimum_fusion
  (9 shorter events, 0.1 us)
Async XLA Ops:
  6.5 484.2 %all-reduce.3.cloned.1.call-start = ((), (), s32[]{:S(2)}) async-start(), calls=%async_computation | async-start | bytes 6291456 | tf_op jit(solution)/shard_map/psum | solution.py:58
  7.3 5.1 collective-permute-start
  251.0 5.8 %copy-start = (f32[128,512,32]{1,0,2:T(8,128)S(1)}, f32[128,512,32]{1,0,2:T(8,128)}, u32[]{:S(2)}) copy-start(f32[128,512,32]{1,0,2:T(8,128)} %copy.26) | copy-start | bytes 25165828
  259.9 92.8 %collective-permute-start.1 = (bf16[32,128,512]{2,1,0:T(8,128)(2,1)S(1)}, bf16[32,128,512]{2,1,0:T(8,128)(2,1)S(1)}, u32[]{:S(2)}, u32[]{:S(2)}) collective-permute-start(bf16[32,128,512]{2,1,0:T(8,128)(2,1)S(1)} %multiply_convert_fusion), channel_id=1, source_target_pairs={{2,0},{4,2},{6,4},{8,6},{10,8},{12,10},{14,12},{16,14},{18,16},{20... | collective-permute-start | bytes 12582920 | tf_op jit(solution)/shard_map/ppermute | solution.py:15
  261.8 95.1 %collective-permute-start.2 = (bf16[32,128,512]{2,1,0:T(8,128)(2,1)S(1)}, bf16[32,128,512]{2,1,0:T(8,128)(2,1)S(1)}, u32[]{:S(2)}, u32[]{:S(2)}) collective-permute-start(bf16[32,128,512]{2,1,0:T(8,128)(2,1)S(1)} %multiply_convert_fusion), channel_id=1, source_target_pairs={{4,0},{6,2},{8,4},{10,6},{12,8},{14,10},{16,12},{18,14},{20,16},{2... | collective-permute-start | bytes 12582920 | tf_op jit(solution)/shard_map/ppermute | solution.py:15
  494.0 7.0 %collective-permute-start.3 = (f32[512]{0:T(512)S(1)}, f32[512]{0:T(512)S(1)}, u32[]{:S(2)}, u32[]{:S(2)}) collective-permute-start(f32[512]{0:T(512)S(1)} %broadcast_subtract_fusion.1), channel_id=1, source_target_pairs={{0,2},{2,4},{4,6},{6,8},{8,10},{10,12},{12,14},{14,16},{16,18},{18... | collective-permute-start | bytes 6152 | tf_op jit(solution)/shard_map/ppermute | solution.py:15
  497.8 5.2 %collective-permute-start.4 = (f32[512]{0:T(512)S(1)}, f32[512]{0:T(512)S(1)}, u32[]{:S(2)}, u32[]{:S(2)}) collective-permute-start(f32[512]{0:T(512)S(1)} %broadcast_subtract_fusion), channel_id=1, source_target_pairs={{0,4},{2,6},{4,8},{6,10},{8,12},{10,14},{12,16},{14,18},{16,20},{1... | collective-permute-start | bytes 6152 | tf_op jit(solution)/shard_map/ppermute | solution.py:15
Sparse Core Ops, SparseCore 0:
  360.4 130.2 all-reduce.2
where the time goes:
time: 511 us; the launch traced here: 510 us
  local copies, waits for them, and re-layouts  240 us (47%)
  waiting for transfers between devices  219 us (43%)
  starting transfers between devices  15.5 us (3%)
  between operations  14.2 us (3%)
  other arithmetic  12.6 us (2%)
  matrix products  10.1 us (2%)
    gather x2, local copies, waits for them, and re-layouts, normalize(): windows = extended[:, starts]  238 us
    psum x1, waiting for transfers between devices, summed(): total = lax.psum(correlate(query, right), 'chan')  130 us
    ppermute x5, waiting for transfers between devices, from_behind(): return lax.ppermute(shard, axis, pairs)  88.8 us
    ppermute x5, starting transfers between devices, from_behind(): return lax.ppermute(shard, axis, pairs)  15.5 us
  transfers between devices with their start and end apart: 6, of which 5 were waited for; matrix products, arithmetic and copies ran while one was open for 1% of the time, Pallas kernels for 0%

commit v1 on v0

--- a/solution.py
+++ b/solution.py
@@ -55,7 +55,7 @@
     row_pos = block_index * count + jnp.arange(count, dtype=jnp.int32)[:, None]
 
     def summed(right, offset):
-        total = lax.psum(correlate(query, right), "chan")
+        total = jnp.sum(lax.all_gather(correlate(query, right), "chan"), axis=0)
         return scored(total, row_pos, offset)
 
     own_scores = summed(query, 0)

time: 511 us -> 464 us (0.908)
  waiting for transfers between devices: 219 us -> 155 us
  matrix products: 10.1 us -> 20.4 us
  other arithmetic: 12.6 us -> 18.6 us
    psum x1 -> x0, waiting for transfers between devices: 130 us -> none  [summed(): total = lax.psum(correlate(query, right), 'chan')]
    all_gather x0 -> x3, waiting for transfers between devices: none -> 70.2 us  [summed(): total = jnp.sum(lax.all_gather(correlate(query, right), 'chan'), axis=0)]
    dot_general x3, matrix products: 10.1 us -> 20.4 us  [correlate(): lax.dot_general(left, right, (((0, 1), (0, 1)), ((), ())), preferred_elem...]
    reduce_sum x0 -> x3, other arithmetic: none -> 5.87 us  [summed(): total = jnp.sum(lax.all_gather(correlate(query, right), 'chan'), axis=0)]
  transfers between devices with their start and end apart: 6 -> 8, of which waited for: 5 -> 5; matrix products, arithmetic and copies ran while one was open for 1% -> 5% of each run, Pallas kernels for 0% -> 0%
where the time goes in v1:
time: 464 us; the launch traced here: 463 us
  local copies, waits for them, and re-layouts  240 us (52%)
  waiting for transfers between devices  155 us (33%)
  matrix products  20.4 us (4%)
  other arithmetic  18.6 us (4%)
  starting transfers between devices  15.5 us (3%)
  between operations  13.9 us (3%)
    gather x2, local copies, waits for them, and re-layouts, normalize(): windows = extended[:, starts]  238 us
    ppermute x5, waiting for transfers between devices, from_behind(): return lax.ppermute(shard, axis, pairs)  84.9 us
    all_gather x3, waiting for transfers between devices, summed(): total = jnp.sum(lax.all_gather(correlate(query, right), 'chan'), axis=0)  70.2 us
    dot_general x3, matrix products, correlate(): lax.dot_general(left, right, (((0, 1), (0, 1)), ((), ())), preferred_elem...  20.4 us
    ppermute x5, starting transfers between devices, from_behind(): return lax.ppermute(shard, axis, pairs)  15.3 us
  transfers between devices with their start and end apart: 8, of which 5 were waited for; matrix products, arithmetic and copies ran while one was open for 5% of the time, Pallas kernels for 0%

profile of v1, /device:TPU:9, one launch (start us, length us, event | category | flops | bytes accessed | tf_op | source)
XLA Modules:
  0.0 463.1 jit_solution(14838472900545766581)
XLA Ops:
  6.5 0.7 slice.3
  7.3 2.6 collective-permute-start
  9.9 0.1 copy.32
  10.0 2.3 collective-permute-done
  12.3 0.8 pad_maximum_fusion
  13.2 0.2 copy.23
  13.4 215.5 %gather_fusion = f32[65536,32]{1,0:T(8,128)} fusion(f32[32,639]{0,1:T(8,128)S(1)} %copy.23, s32[65536]{0:T(1024)S(1)} %broadcast_clamp_fusion), kind=kCustom, calls=%fused_computation | custom fusion | bytes 17039360 | tf_op jit(solution)/shard_map/gather | solution.py:22
  228.9 22.1 %copy.31 = f32[128,512,32]{1,0,2:T(8,128)} copy(f32[128,512,32]{2,1,0:T(8,128)} %bitcast.29) | data formatting | bytes 16777216 | tf_op jit(solution)/shard_map/gather | solution.py:22
  251.0 4.7 %bitcast_reduce_fusion = f32[32,512]{1,0:T(8,128)S(1)} fusion(f32[128,512,32]{1,0,2:T(8,128)} %copy.31), kind=kLoop, calls=%fused_computation.1 | loop fusion | flops 2080768 | bytes 8454144 | tf_op jit(solution)/shard_map/reduce_sum | solution.py:23
  255.7 1.0 copy-done
  256.7 1.4 multiply_reduce_fusion
  258.2 3.6 multiply_convert_fusion
  261.9 1.9 collective-permute-start.1
  263.8 3.9 collective-permute-start.2
  267.6 6.8 %convolution_bitcast_fusion.2 = f32[512,512]{1,0:T(8,128)} fusion(bf16[32,128,512]{2,1,0:T(8,128)(2,1)} %multiply_convert_fusion), kind=kOutput, calls=%fused_computation.7 | convolution fusion | flops 2147483648 | bytes 5242880 | tf_op jit(solution)/shard_map/dot_general | solution.py:31
  274.5 0.0 all-gather.7.cloned.1.call-update
  274.5 0.0 all-gather.9.cloned.1.call-start
  274.5 80.4 %collective-permute-done.1 = bf16[32,128,512]{2,1,0:T(8,128)(2,1)} collective-permute-done((bf16[32,128,512]{2,1,0:T(8,128)(2,1)}, bf16[32,128,512]{2,1,0:T(8,128)(2,1)}, u32[]{:S(2)}, u32[]{:S(2)}) %collective-permute-start.1) | collective-permute-done | bytes 4194336 | tf_op jit(solution)/shard_map/ppermute | solution.py:15
  354.9 6.8 %convolution_bitcast_fusion.1 = f32[512,512]{1,0:T(8,128)} fusion(bf16[32,128,512]{2,1,0:T(8,128)(2,1)} %multiply_convert_fusion, bf16[32,128,512]{2,1,0:T(8,128)(2,1)} %collective-permute-done.1), kind=kOutput, calls=%fused_computation.6 | convolution fusion | flops 2147483648 | bytes 9437184 | tf_op jit(solution)/shard_map/dot_general | solution.py:31
  361.8 0.2 all-gather.11.cloned.1.call-start
  362.0 6.8 %convolution_bitcast_fusion = f32[512,512]{1,0:T(8,128)} fusion(bf16[32,128,512]{2,1,0:T(8,128)(2,1)} %multiply_convert_fusion, bf16[32,128,512]{2,1,0:T(8,128)(2,1)} %collective-permute-done.2), kind=kOutput, calls=%fused_computation.5 | convolution fusion | flops 2147483648 | bytes 9437184 | tf_op jit(solution)/shard_map/dot_general | solution.py:31
  369.5 0.0 all-gather.7.cloned.1.call-done
  369.6 2.1 reduce_sum.47
  371.6 25.2 %all-gather.9.cloned.1.call-done = f32[1024,512]{1,0:T(8,128)} async-done(((f32[512,512]{1,0:T(8,128)}), f32[1024,512]{1,0:T(8,128)}) %all-gather.9.cloned.1.call-update) | async-done | bytes 2097168 | tf_op jit(solution)/shard_map/all_gather | solution.py:58
  396.9 1.9 reduce_sum.48
  398.8 44.9 %all-gather.11.cloned.1.call-done = f32[1024,512]{1,0:T(8,128)} async-done(((f32[512,512]{1,0:T(8,128)}), f32[1024,512]{1,0:T(8,128)}) %all-gather.11.cloned.1.call-update) | async-done | bytes 2097168 | tf_op jit(solution)/shard_map/all_gather | solution.py:58
  443.7 1.9 reduce_sum.49
  445.6 1.3 fusion.6
  446.9 3.8 collective-permute-start.3
  450.8 3.1 collective-permute-start.4
  453.9 2.1 collective-permute-done.4
  456.0 0.6 minimum_minimum_fusion
  (15 shorter events, 0.1 us)
Async XLA Ops:
  6.5 363.0 %all-gather.7.cloned.1.call-start = ((), (), s32[]{:S(2)}) async-start(), calls=%async_computation | async-start | bytes 3145728 | tf_op jit(solution)/shard_map/all_gather | solution.py:58
  7.3 5.1 %collective-permute-start = (f32[32,127]{1,0:T(8,128)S(1)}, f32[32,127]{1,0:T(8,128)S(1)}, u32[]{:S(2)}, u32[]{:S(2)}) collective-permute-start(f32[32,127]{1,0:T(8,128)S(1)} %slice.3), channel_id=1, source_target_pairs={{2,0},{4,2},{6,4},{8,6},{10,8},{12,10},{14,12},{16,14},{18,16},{20... | collective-permute-start | bytes 48776 | tf_op jit(solution)/shard_map/ppermute | solution.py:15
  251.0 5.8 %copy-start = (f32[128,512,32]{1,0,2:T(8,128)S(1)}, f32[128,512,32]{1,0,2:T(8,128)}, u32[]{:S(2)}) copy-start(f32[128,512,32]{1,0,2:T(8,128)} %copy.31) | copy-start | bytes 25165828
  261.9 93.1 %collective-permute-start.1 = (bf16[32,128,512]{2,1,0:T(8,128)(2,1)}, bf16[32,128,512]{2,1,0:T(8,128)(2,1)}, u32[]{:S(2)}, u32[]{:S(2)}) collective-permute-start(bf16[32,128,512]{2,1,0:T(8,128)(2,1)} %multiply_convert_fusion), channel_id=1, source_target_pairs={{2,0},{4,2},{6,4},{8,6},{10,8},{12,10},{14,12},{16,14},{18,16},{20... | collective-permute-start | bytes 12582920 | tf_op jit(solution)/shard_map/ppermute | solution.py:15
  263.8 98.2 %collective-permute-start.2 = (bf16[32,128,512]{2,1,0:T(8,128)(2,1)}, bf16[32,128,512]{2,1,0:T(8,128)(2,1)}, u32[]{:S(2)}, u32[]{:S(2)}) collective-permute-start(bf16[32,128,512]{2,1,0:T(8,128)(2,1)} %multiply_convert_fusion), channel_id=1, source_target_pairs={{4,0},{6,2},{8,4},{10,6},{12,8},{14,10},{16,12},{18,14},{20,16},{2... | collective-permute-start | bytes 12582920 | tf_op jit(solution)/shard_map/ppermute | solution.py:15
  274.5 122.4 %all-gather.9.cloned.1.call-start = ((), (), s32[]{:S(2)}) async-start(), calls=%async_computation.1 | async-start | bytes 3145728 | tf_op jit(solution)/shard_map/all_gather | solution.py:58
  361.8 81.9 %all-gather.11.cloned.1.call-start = ((), (), s32[]{:S(2)}) async-start(), calls=%async_computation.2 | async-start | bytes 3145728 | tf_op jit(solution)/shard_map/all_gather | solution.py:58
  446.9 7.0 %collective-permute-start.3 = (f32[512]{0:T(512)S(1)}, f32[512]{0:T(512)S(1)}, u32[]{:S(2)}, u32[]{:S(2)}) collective-permute-start(f32[512]{0:T(512)S(1)} %broadcast_subtract_fusion.1), channel_id=1, source_target_pairs={{0,2},{2,4},{4,6},{6,8},{8,10},{10,12},{12,14},{14,16},{16,18},{18... | collective-permute-start | bytes 6152 | tf_op jit(solution)/shard_map/ppermute | solution.py:15
  450.8 5.2 %collective-permute-start.4 = (f32[512]{0:T(512)S(1)}, f32[512]{0:T(512)S(1)}, u32[]{:S(2)}, u32[]{:S(2)}) collective-permute-start(f32[512]{0:T(512)S(1)} %broadcast_subtract_fusion), channel_id=1, source_target_pairs={{0,4},{2,6},{4,8},{6,10},{8,12},{10,14},{12,16},{14,18},{16,20},{1... | collective-permute-start | bytes 6152 | tf_op jit(solution)/shard_map/ppermute | solution.py:15
Sparse Core Ops, SparseCore 0:
  274.6 36.2 all-gather.6
  361.9 34.9 all-gather.8
  398.4 45.2 all-gather.10
